TPU v7x, 256 devices: a whole 4x4x8 slice. The times are simulated.
256 devices in a mesh: row: 32 (over x, z), col: 8 (over y, core).
Axes of the slice: x: 4, y: 4, z: 8, core: 2. Of those that a mesh axis runs over, the one named last changes fastest.
Arguments:
- panel_block: float32 [16384, 128], P('row'), may hold values from -8 to 8, as said below
- trailing: float32 [16384, 16384], P('row', 'col'), may hold values from -80 to 80
Outputs:
- reduced: float32 [16384, 16384], P('row', 'col')
- band_block: float32 [128, 128], replicated
- first_factor: float32 [128, 128], replicated
Inputs may be any that keep to these rules, and one draw needn't show every extreme that they name: `panel_block`: entries of order the inverse square root of 16384; rows may differ in scale; the columns may be nearly dependent, with a condition number of the panel up to a few thousand; the first 128 rows of the orthonormal basis have spectral norm at most 0.8, so that I + top^T needs no pivoting.
All inputs are finite; a program needn't handle non-finite values.
Results may differ from a plain program's by a relative error of at most 0.0017.
Values sent between devices are 32-bit elements; how exact they have to be, the bound alone decides.
A program may use at most 128 MiB of HBM per device.

v0:
```python
import jax
import jax.numpy as jnp
from jax import lax
from jax.sharding import PartitionSpec as P

HIGH = lax.Precision.HIGHEST


def broadcast(shard, axis, root):
    mine = lax.axis_index(axis) == root
    return lax.psum(jnp.where(mine, shard, jnp.zeros_like(shard)), axis)


def gram_of(values):
    return lax.dot_general(
        values, values, (((0,), (0,)), ((), ())), precision=HIGH, preferred_element_type=jnp.float32
    )


def times_of(left, right):
    return jnp.dot(left, right, precision=HIGH, preferred_element_type=jnp.float32)


def outer_of(left, right):
    return lax.dot_general(
        left, right, (((1,), (1,)), ((), ())), precision=HIGH, preferred_element_type=jnp.float32
    )


def gram_both(left, right):
    return lax.dot_general(
        left, right, (((0,), (0,)), ((), ())), precision=HIGH, preferred_element_type=jnp.float32
    )


def eliminate_small(square):
    size_n = square.shape[0]
    augmented = jnp.concatenate([square, jnp.eye(size_n, dtype=square.dtype)], axis=1)
    positions = jnp.arange(size_n)

    def eliminate(pivot, current):
        pivot_row = lax.dynamic_index_in_dim(current, pivot, 0, keepdims=False)
        pivot_row = pivot_row / pivot_row[pivot]
        column = lax.dynamic_index_in_dim(current, pivot, 1, keepdims=False)
        column = column - (positions == pivot).astype(current.dtype)
        return current - column[:, None] * pivot_row[None, :]

    augmented = lax.fori_loop(0, size_n, eliminate, augmented)
    return augmented[:, size_n:]


def invert_square(square):
    size_n = square.shape[0]
    if size_n <= 16:
        return eliminate_small(square)
    half = size_n // 2
    upper_left = square[:half, :half]
    upper_right = square[:half, half:]
    lower_left = square[half:, :half]
    lower_right = square[half:, half:]
    left_inverse = invert_square(upper_left)
    left_times_right = times_of(left_inverse, upper_right)
    lower_times_left = times_of(lower_left, left_inverse)
    schur = lower_right - times_of(lower_left, left_times_right)
    schur_inverse = invert_square(schur)
    top_right = -times_of(left_times_right, schur_inverse)
    bottom_left = -times_of(schur_inverse, lower_times_left)
    top_left = left_inverse - times_of(top_right, lower_times_left)
    upper = jnp.concatenate([top_left, top_right], axis=1)
    lower = jnp.concatenate([bottom_left, schur_inverse], axis=1)
    return jnp.concatenate([upper, lower], axis=0)


def right_solve(factor, values):
    return lax.linalg.triangular_solve(
        factor, values, left_side=False, lower=True, transpose_a=True
    )


def body(panel_block, trailing):
    shard_rows = panel_block.shape[0]
    panel_width = panel_block.shape[1]
    col_count = trailing.shape[1]
    row_index = lax.axis_index("row")
    col_index = lax.axis_index("col")
    first_gram = lax.psum(gram_of(panel_block), "row")
    first_factor = jnp.linalg.cholesky(first_gram)
    first_basis = right_solve(first_factor, panel_block)
    second_gram = lax.psum(gram_of(first_basis), "row")
    second_factor = jnp.linalg.cholesky(second_gram)
    basis = right_solve(second_factor, first_basis)
    top_basis = broadcast(basis[:panel_width], "row", 0)
    band_block = -times_of(second_factor.T, first_factor.T)
    kernel = invert_square(jnp.eye(panel_width, dtype=jnp.float32) + top_basis.T)
    global_rows = row_index * shard_rows + jnp.arange(shard_rows)
    ident = (global_rows[:, None] == jnp.arange(panel_width)[None, :]).astype(jnp.float32)
    vectors = basis + ident
    all_vectors = lax.all_gather(vectors, "row", axis=0, tiled=True)
    col_vectors = lax.dynamic_slice_in_dim(all_vectors, col_index * col_count, col_count, 0)
    partial_product = times_of(trailing, col_vectors)
    row_product = lax.psum(partial_product, "col")
    applied = times_of(row_product, kernel)
    inner_sum = lax.psum(gram_both(vectors, applied), "row")
    inner = times_of(kernel.T, inner_sum)
    row_update = applied - 0.5 * times_of(vectors, inner)
    all_update = lax.all_gather(row_update, "row", axis=0, tiled=True)
    col_update = lax.dynamic_slice_in_dim(all_update, col_index * col_count, col_count, 0)
    reduced = trailing - outer_of(vectors, col_update) - outer_of(row_update, col_vectors)
    return (reduced, band_block, first_factor)


def solution(mesh):
    in_specs = (P("row", None), P("row", "col"))
    out_specs = (P("row", "col"), P(), P())
    return jax.shard_map(body, mesh=mesh, in_specs=in_specs, out_specs=out_specs, check_vma=False)
```

profile of v0, /device:TPU:1, one launch (start us, length us, event | category | flops | bytes accessed | tf_op | source)
XLA Modules:
  0.0 1025.3 jit_solution(8369350252822602380)
XLA Ops:
  7.2 0.9 copy-done
  8.1 1.2 fusion.134
  9.4 143.5 %all-reduce.6.cloned.1.call-done = f32[128,128]{0,1:T(8,128)} async-done(((f32[128,128]{0,1:T(8,128)}), f32[128,128]{0,1:T(8,128)}) %all-reduce.6.cloned.1.call-update) | async-done | bytes 65552 | tf_op jit(solution)/shard_map/psum | solution.py:86
  152.9 0.9 copy.26
  153.9 0.9 fusion.57
  154.7 11.7 %cholesky.44 = f32[128,128]{1,0:T(8,128)S(1)} custom-call(f32[128,128]{1,0:T(8,128)S(1)} %fusion.57), custom_call_target="Cholesky" | custom-call | tf_op jit(solution)/shard_map/jit(cholesky)/cholesky | solution.py:87
  167.8 9.8 custom-call.6
  178.0 1.0 fusion.135
  179.3 139.5 %all-reduce.8.cloned.1.call-done = f32[128,128]{0,1:T(8,128)} async-done(((f32[128,128]{0,1:T(8,128)}), f32[128,128]{0,1:T(8,128)}) %all-reduce.8.cloned.1.call-update) | async-done | bytes 65552 | tf_op jit(solution)/shard_map/psum | solution.py:89
  318.8 0.9 copy.28
  319.7 0.9 fusion.55
  320.6 11.7 %cholesky.55 = f32[128,128]{1,0:T(8,128)S(1)} custom-call(f32[128,128]{1,0:T(8,128)S(1)} %fusion.55), custom_call_target="Cholesky" | custom-call | tf_op jit(solution)/shard_map/jit(cholesky)/cholesky | solution.py:90
  333.5 9.8 custom-call.7
  343.3 1.1 convert_add_fusion
  346.0 138.9 %all-reduce.12.cloned.1.call-done = f32[128,128]{1,0:T(8,128)} async-done(((f32[128,128]{1,0:T(8,128)}), f32[128,128]{1,0:T(8,128)}) %all-reduce.12.cloned.1.call-update) | async-done | bytes 65552 | tf_op jit(solution)/shard_map/psum | solution.py:11
  484.9 0.9 fusion.65
  485.9 24.0 %while.136 = (s32[]{:T(128)}, f32[16,32]{0,1:T(8,128)S(1)}, s32[]{:T(128)}, s32[]{:T(128)}, s32[]{:T(128)}, /*index=5*/s32[]{:T(128)}) while((s32[]{:T(128)}, f32[16,32]{0,1:T(8,128)S(1)}, s32[]{:T(128)}, s32[]{:T(128)}, s32[]{:T(128)}, /*index=5*/s32[]{:T(128)}) %tuple.325), condition=%wide.region_7.10_spmd.clone, body=%wide.region_6.9_spmd.clone.sunk | while | flops 1108 | bytes 5825 | solution.py:48
  501.5 0.8 fusion.206
  503.0 0.8 fusion.206
  506.0 0.8 fusion.206
  509.1 0.8 fusion.206
  510.8 24.0 %while.137 = (s32[]{:T(128)}, f32[16,32]{0,1:T(8,128)S(1)}, s32[]{:T(128)}, s32[]{:T(128)}, s32[]{:T(128)}, /*index=5*/s32[]{:T(128)}) while((s32[]{:T(128)}, f32[16,32]{0,1:T(8,128)S(1)}, s32[]{:T(128)}, s32[]{:T(128)}, s32[]{:T(128)}, /*index=5*/s32[]{:T(128)}) %tuple.328), condition=%wide.region_9.12_spmd.clone, body=%wide.region_8.11_spmd.clone.sunk | while | flops 1108 | bytes 5825 | solution.py:48
  515.8 0.8 fusion.208
  520.3 0.8 fusion.208
  521.8 0.8 fusion.208
  536.2 24.0 %while.138 = (s32[]{:T(128)}, f32[16,32]{0,1:T(8,128)S(1)}, s32[]{:T(128)}, s32[]{:T(128)}, s32[]{:T(128)}, /*index=5*/s32[]{:T(128)}) while((s32[]{:T(128)}, f32[16,32]{0,1:T(8,128)S(1)}, s32[]{:T(128)}, s32[]{:T(128)}, s32[]{:T(128)}, /*index=5*/s32[]{:T(128)}) %tuple.331), condition=%wide.region_11.14_spmd.clone, body=%wide.region_10.13_spmd.clone.sunk | while | flops 1108 | bytes 5825 | solution.py:48
  539.8 0.8 fusion.210
  541.3 0.8 fusion.210
  553.4 0.8 fusion.210
  556.4 0.8 fusion.210
  561.1 24.0 %while.139 = (s32[]{:T(128)}, f32[16,32]{0,1:T(8,128)S(1)}, s32[]{:T(128)}, s32[]{:T(128)}, s32[]{:T(128)}, /*index=5*/s32[]{:T(128)}) while((s32[]{:T(128)}, f32[16,32]{0,1:T(8,128)S(1)}, s32[]{:T(128)}, s32[]{:T(128)}, s32[]{:T(128)}, /*index=5*/s32[]{:T(128)}) %tuple.334), condition=%wide.region_13.16_spmd.clone, body=%wide.region_12.15_spmd.clone.sunk | while | flops 1108 | bytes 5825 | solution.py:48
  561.7 0.8 fusion.212
  567.7 0.8 fusion.212
  587.1 24.0 %while.140 = (s32[]{:T(128)}, f32[16,32]{0,1:T(8,128)S(1)}, s32[]{:T(128)}, s32[]{:T(128)}, s32[]{:T(128)}, /*index=5*/s32[]{:T(128)}) while((s32[]{:T(128)}, f32[16,32]{0,1:T(8,128)S(1)}, s32[]{:T(128)}, s32[]{:T(128)}, s32[]{:T(128)}, /*index=5*/s32[]{:T(128)}) %tuple.337), condition=%wide.region_15.18_spmd.clone, body=%wide.region_14.17_spmd.clone.sunk | while | flops 1108 | bytes 5825 | solution.py:48
  611.7 24.0 %while.141 = (s32[]{:T(128)}, f32[16,32]{0,1:T(8,128)S(1)}, s32[]{:T(128)}, s32[]{:T(128)}, s32[]{:T(128)}, /*index=5*/s32[]{:T(128)}) while((s32[]{:T(128)}, f32[16,32]{0,1:T(8,128)S(1)}, s32[]{:T(128)}, s32[]{:T(128)}, s32[]{:T(128)}, /*index=5*/s32[]{:T(128)}) %tuple.340), condition=%wide.region_17.20_spmd.clone, body=%wide.region_16.19_spmd.clone.sunk | while | flops 1108 | bytes 5825 | solution.py:48
  637.1 24.0 %while.142 = (s32[]{:T(128)}, f32[16,32]{0,1:T(8,128)S(1)}, s32[]{:T(128)}, s32[]{:T(128)}, s32[]{:T(128)}, /*index=5*/s32[]{:T(128)}) while((s32[]{:T(128)}, f32[16,32]{0,1:T(8,128)S(1)}, s32[]{:T(128)}, s32[]{:T(128)}, s32[]{:T(128)}, /*index=5*/s32[]{:T(128)}) %tuple.343), condition=%wide.region_19.22_spmd.clone, body=%wide.region_18.21_spmd.clone.sunk | while | flops 1108 | bytes 5825 | solution.py:48
  661.7 24.0 %while.143 = (s32[]{:T(128)}, f32[16,32]{0,1:T(8,128)S(1)}, s32[]{:T(128)}, s32[]{:T(128)}, s32[]{:T(128)}, /*index=5*/s32[]{:T(128)}) while((s32[]{:T(128)}, f32[16,32]{0,1:T(8,128)S(1)}, s32[]{:T(128)}, s32[]{:T(128)}, s32[]{:T(128)}, /*index=5*/s32[]{:T(128)}) %tuple.346), condition=%wide.region_21.24_spmd.clone, body=%wide.region_20.23_spmd.clone.sunk | while | flops 1108 | bytes 5825 | solution.py:48
  688.1 7.6 convolution_bitcast_fusion
  696.0 65.7 %all-reduce.10.cloned.1.call-done = f32[512,128]{0,1:T(8,128)} async-done(((f32[512,128]{0,1:T(8,128)}), f32[512,128]{0,1:T(8,128)}) %all-reduce.10.cloned.1.call-update) | async-done | bytes 262160 | tf_op jit(solution)/shard_map/psum | solution.py:101
  761.7 1.6 fusion.132
  763.3 1.0 fusion.136
  764.6 139.2 %all-reduce.14.cloned.1.call-done = f32[128,128]{1,0:T(8,128)} async-done(((f32[128,128]{1,0:T(8,128)}), f32[128,128]{1,0:T(8,128)}) %all-reduce.14.cloned.1.call-update) | async-done | bytes 65552 | tf_op jit(solution)/shard_map/psum | solution.py:103
  903.9 1.2 fusion.131
  905.1 1.3 fusion.48
  906.4 1.5 convolution_negate_fusion
  907.9 98.7 %all-gather.5.cloned.1.call-done = f32[16384,128]{1,0:T(8,128)} async-done(((f32[512,128]{1,0:T(8,128)}), f32[16384,128]{1,0:T(8,128)}) %all-gather.5.cloned.1.call-update) | async-done | bytes 8388624 | tf_op jit(solution)/shard_map/all_gather | solution.py:106
  1006.7 5.0 fusion.49
  1011.7 6.7 subtract_subtract_fusion
  (608 shorter events, 195.8 us)
Async XLA Ops:
  7.2 1.0 copy-start
  7.2 145.8 %all-reduce.6.cloned.1.call-start = ((), (), s32[]{:S(2)}) async-start(), calls=%async_computation | async-start | bytes 131072 | tf_op jit(solution)/shard_map/psum | solution.py:86
  9.4 309.4 %all-reduce.8.cloned.1.call-start = ((), (), s32[]{:S(2)}) async-start(), calls=%async_computation.1 | async-start | bytes 131072 | tf_op jit(solution)/shard_map/psum | solution.py:89
  167.8 738.6 %copy-start.4 = (f32[128,128]{1,0:T(8,128)}, f32[128,128]{1,0:T(8,128)S(1)}, u32[]{:S(2)}) copy-start(f32[128,128]{1,0:T(8,128)S(1)} %get-tuple-element.926) | copy-start | bytes 196612
  179.1 305.8 %all-reduce.12.cloned.1.call-start = ((), (), s32[]{:S(2)}) async-start(), calls=%async_computation.4 | async-start | bytes 131072 | tf_op jit(solution)/shard_map/psum | solution.py:11
  345.1 343.0 %all-gather.3.cloned.1.call-start = ((), (), s32[]{:S(2)}) async-start(), calls=%async_computation.2 | async-start | bytes 8650752 | tf_op jit(solution)/shard_map/all_gather | solution.py:98
  345.7 416.0 %all-reduce.10.cloned.1.call-start = ((), (), s32[]{:S(2)}) async-start(), calls=%async_computation.3 | async-start | bytes 524288 | tf_op jit(solution)/shard_map/psum | solution.py:101
  637.1 126.1 %copy-start.2 = (f32[512,128]{0,1:T(8,128)S(1)}, f32[512,128]{0,1:T(8,128)}, u32[]{:S(2)}) copy-start(f32[512,128]{0,1:T(8,128)} %get-tuple-element.927) | copy-start | bytes 786436
  695.7 208.2 %all-reduce.14.cloned.1.call-start = ((), (), s32[]{:S(2)}) async-start(), calls=%async_computation.5 | async-start | bytes 131072 | tf_op jit(solution)/shard_map/psum | solution.py:103
  764.3 242.3 %all-gather.5.cloned.1.call-start = ((), (), s32[]{:S(2)}) async-start(), calls=%async_computation.6 | async-start | bytes 8650752 | tf_op jit(solution)/shard_map/all_gather | solution.py:106
  906.4 105.3 %copy-start.3 = (f32[512,128]{1,0:T(8,128)S(1)}, f32[512,128]{1,0:T(8,128)}, u32[]{:S(2)}) copy-start(f32[512,128]{1,0:T(8,128)} %fusion.48) | copy-start | bytes 786436
  1006.7 5.1 copy-start.1
Sparse Core Ops, SparseCore 0:
  12.0 140.8 all-reduce.5
  179.2 139.5 all-reduce.7
  345.3 139.6 all-reduce.11
  487.9 100.0 all-gather.2
  695.8 65.7 all-reduce.9
  765.6 138.2 all-reduce.13
  907.0 99.5 all-gather.4
where the time goes:
time: 1030 us
  waiting for transfers between devices  726 us (70%)
  other arithmetic  166 us (16%)
  local copies, waits for them, and re-layouts  79.2 us (8%)
  matrix products  37.4 us (4%)
  between operations  14.5 us (1%)
    psum x1, waiting for transfers between devices, body(): first_gram = lax.psum(gram_of(panel_block), 'row')  144 us
    psum x1, waiting for transfers between devices, body(): second_gram = lax.psum(gram_of(first_basis), 'row')  139 us
    psum x1, waiting for transfers between devices, body(): inner_sum = lax.psum(gram_both(vectors, applied), 'row')  139 us
    psum x1, waiting for transfers between devices, broadcast(): return lax.psum(jnp.where(mine, shard, jnp.zeros_like(shard)), axis)  139 us
    div x128, other arithmetic, eliminate(): pivot_row = pivot_row / pivot_row[pivot]  106 us
    all_gather x1, waiting for transfers between devices, body(): all_update = lax.all_gather(row_update, 'row', axis=0, tiled=True)  98.7 us
    dynamic_slice x128, local copies, waits for them, and re-layouts, eliminate(): pivot_row = pivot_row / pivot_row[pivot]  74.9 us
    psum x1, waiting for transfers between devices, body(): row_product = lax.psum(partial_product, 'col')  65.7 us
  transfers between devices with their start and end apart: 7, of which 6 were waited for; matrix products, arithmetic and copies ran while one was open for 20% of the time, Pallas kernels for 0%

commit v1 on v0

--- a/solution.py
+++ b/solution.py
@@ -98,7 +98,11 @@
     all_vectors = lax.all_gather(vectors, "row", axis=0, tiled=True)
     col_vectors = lax.dynamic_slice_in_dim(all_vectors, col_index * col_count, col_count, 0)
     partial_product = times_of(trailing, col_vectors)
-    row_product = lax.psum(partial_product, "col")
+    row_product = partial_product
+    for hop in (1, 2, 4):
+        row_product = row_product + lax.ppermute(
+            row_product, "col", [(dev, dev ^ hop) for dev in range(8)]
+        )
     applied = times_of(row_product, kernel)
     inner_sum = lax.psum(gram_both(vectors, applied), "row")
     inner = times_of(kernel.T, inner_sum)

time: 1030 us -> 978 us (0.950)
  waiting for transfers between devices: 726 us -> 669 us
    psum x1 -> x0, waiting for transfers between devices: 65.7 us -> none  [body(): row_product = lax.psum(partial_product, 'col')]
    ppermute x0 -> x3, waiting for transfers between devices: none -> 11.7 us  [body(): lax.ppermute(row_product, 'col', [(dev, dev ^ hop) for dev in range(8)])]
  transfers between devices with their start and end apart: 7 -> 9, of which waited for: 6 -> 8; matrix products, arithmetic and copies ran while one was open for 20% -> 21% of each run, Pallas kernels for 0% -> 0%
where the time goes in v1:
time: 978 us; the launch traced here: 976 us
  waiting for transfers between devices  669 us (68%)
  other arithmetic  166 us (17%)
  local copies, waits for them, and re-layouts  79.2 us (8%)
  matrix products  35.7 us (4%)
  between operations  14.5 us (1%)
  starting transfers between devices  10.1 us (1%)
    psum x1, waiting for transfers between devices, body(): first_gram = lax.psum(gram_of(panel_block), 'row')  144 us
    psum x1, waiting for transfers between devices, body(): second_gram = lax.psum(gram_of(first_basis), 'row')  139 us
    psum x1, waiting for transfers between devices, broadcast(): return lax.psum(jnp.where(mine, shard, jnp.zeros_like(shard)), axis)  139 us
    psum x1, waiting for transfers between devices, body(): inner_sum = lax.psum(gram_both(vectors, applied), 'row')  137 us
    div x128, other arithmetic, eliminate(): pivot_row = pivot_row / pivot_row[pivot]  106 us
    all_gather x1, waiting for transfers between devices, body(): all_update = lax.all_gather(row_update, 'row', axis=0, tiled=True)  98.6 us
    dynamic_slice x128, local copies, waits for them, and re-layouts, eliminate(): pivot_row = pivot_row / pivot_row[pivot]  74.9 us
    another operation x4, other arithmetic, right_solve(): lax.linalg.triangular_solve(factor, values, left_side=False, lower=True,...  20.8 us
  transfers between devices with their start and end apart: 9, of which 8 were waited for; matrix products, arithmetic and copies ran while one was open for 21% of the time, Pallas kernels for 0%

profile of v1, /device:TPU:1, one launch (start us, length us, event | category | flops | bytes accessed | tf_op | source)
XLA Modules:
  0.0 976.0 jit_solution(390528649271397668)
XLA Ops:
  7.2 0.9 copy-done
  8.1 1.2 fusion.135
  9.4 143.5 %all-reduce.5.cloned.1.call-done = f32[128,128]{0,1:T(8,128)} async-done(((f32[128,128]{0,1:T(8,128)}), f32[128,128]{0,1:T(8,128)}) %all-reduce.5.cloned.1.call-update) | async-done | bytes 65552 | tf_op jit(solution)/shard_map/psum | solution.py:86
  152.9 0.9 copy.26
  153.9 0.9 fusion.59
  154.7 11.7 %cholesky.44 = f32[128,128]{1,0:T(8,128)S(1)} custom-call(f32[128,128]{1,0:T(8,128)S(1)} %fusion.59), custom_call_target="Cholesky" | custom-call | tf_op jit(solution)/shard_map/jit(cholesky)/cholesky | solution.py:87
  167.8 9.8 %custom-call.6 = f32[1,128,128]{1,2,0:T(8,128)S(1)} custom-call(f32[1,128,128]{2,1,0:T(8,128)S(1)} %get-tuple-element.925), custom_call_target="InvertDiagBlocksLowerTriangular" | custom-call | tf_op jit(solution)/shard_map/triangular_solve/custom-call.0 | solution.py:75
  178.0 1.0 fusion.136
  179.3 139.5 %all-reduce.7.cloned.1.call-done = f32[128,128]{0,1:T(8,128)} async-done(((f32[128,128]{0,1:T(8,128)}), f32[128,128]{0,1:T(8,128)}) %all-reduce.7.cloned.1.call-update) | async-done | bytes 65552 | tf_op jit(solution)/shard_map/psum | solution.py:89
  318.8 0.9 copy.28
  319.7 0.9 fusion.57
  320.6 11.7 %cholesky.55 = f32[128,128]{1,0:T(8,128)S(1)} custom-call(f32[128,128]{1,0:T(8,128)S(1)} %fusion.57), custom_call_target="Cholesky" | custom-call | tf_op jit(solution)/shard_map/jit(cholesky)/cholesky | solution.py:90
  333.5 9.8 %custom-call.7 = f32[1,128,128]{1,2,0:T(8,128)S(1)} custom-call(f32[1,128,128]{2,1,0:T(8,128)S(1)} %select_bitcast_fusion), custom_call_target="InvertDiagBlocksLowerTriangular" | custom-call | tf_op jit(solution)/shard_map/triangular_solve/custom-call.0 | solution.py:75
  343.3 1.1 convert_add_fusion
  346.0 138.9 %all-reduce.9.cloned.1.call-done = f32[128,128]{1,0:T(8,128)} async-done(((f32[128,128]{1,0:T(8,128)}), f32[128,128]{1,0:T(8,128)}) %all-reduce.9.cloned.1.call-update) | async-done | bytes 65552 | tf_op jit(solution)/shard_map/psum | solution.py:11
  484.9 0.9 fusion.67
  485.9 24.0 %while.136 = (s32[]{:T(128)}, f32[16,32]{0,1:T(8,128)S(1)}, s32[]{:T(128)}, s32[]{:T(128)}, s32[]{:T(128)}, /*index=5*/s32[]{:T(128)}) while((s32[]{:T(128)}, f32[16,32]{0,1:T(8,128)S(1)}, s32[]{:T(128)}, s32[]{:T(128)}, s32[]{:T(128)}, /*index=5*/s32[]{:T(128)}) %tuple.325), condition=%wide.region_6.9_spmd.clone, body=%wide.region_5.8_spmd.clone.sunk | while | flops 1108 | bytes 5825 | solution.py:48
  501.5 0.8 fusion.206
  506.0 0.8 fusion.206
  509.1 0.8 fusion.206
  510.8 24.0 %while.137 = (s32[]{:T(128)}, f32[16,32]{0,1:T(8,128)S(1)}, s32[]{:T(128)}, s32[]{:T(128)}, s32[]{:T(128)}, /*index=5*/s32[]{:T(128)}) while((s32[]{:T(128)}, f32[16,32]{0,1:T(8,128)S(1)}, s32[]{:T(128)}, s32[]{:T(128)}, s32[]{:T(128)}, /*index=5*/s32[]{:T(128)}) %tuple.328), condition=%wide.region_8.11_spmd.clone, body=%wide.region_7.10_spmd.clone.sunk | while | flops 1108 | bytes 5825 | solution.py:48
  515.8 0.8 fusion.208
  520.3 0.8 fusion.208
  536.2 24.0 %while.138 = (s32[]{:T(128)}, f32[16,32]{0,1:T(8,128)S(1)}, s32[]{:T(128)}, s32[]{:T(128)}, s32[]{:T(128)}, /*index=5*/s32[]{:T(128)}) while((s32[]{:T(128)}, f32[16,32]{0,1:T(8,128)S(1)}, s32[]{:T(128)}, s32[]{:T(128)}, s32[]{:T(128)}, /*index=5*/s32[]{:T(128)}) %tuple.331), condition=%wide.region_10.13_spmd.clone, body=%wide.region_9.12_spmd.clone.sunk | while | flops 1108 | bytes 5825 | solution.py:48
  539.8 0.8 fusion.210
  541.3 0.8 fusion.210
  553.4 0.8 fusion.210
  556.4 0.8 fusion.210
  561.1 24.0 %while.139 = (s32[]{:T(128)}, f32[16,32]{0,1:T(8,128)S(1)}, s32[]{:T(128)}, s32[]{:T(128)}, s32[]{:T(128)}, /*index=5*/s32[]{:T(128)}) while((s32[]{:T(128)}, f32[16,32]{0,1:T(8,128)S(1)}, s32[]{:T(128)}, s32[]{:T(128)}, s32[]{:T(128)}, /*index=5*/s32[]{:T(128)}) %tuple.334), condition=%wide.region_12.15_spmd.clone, body=%wide.region_11.14_spmd.clone.sunk | while | flops 1108 | bytes 5825 | solution.py:48
  567.7 0.8 fusion.212
  587.1 24.0 %while.140 = (s32[]{:T(128)}, f32[16,32]{0,1:T(8,128)S(1)}, s32[]{:T(128)}, s32[]{:T(128)}, s32[]{:T(128)}, /*index=5*/s32[]{:T(128)}) while((s32[]{:T(128)}, f32[16,32]{0,1:T(8,128)S(1)}, s32[]{:T(128)}, s32[]{:T(128)}, s32[]{:T(128)}, /*index=5*/s32[]{:T(128)}) %tuple.337), condition=%wide.region_14.17_spmd.clone, body=%wide.region_13.16_spmd.clone.sunk | while | flops 1108 | bytes 5825 | solution.py:48
  611.7 24.0 %while.141 = (s32[]{:T(128)}, f32[16,32]{0,1:T(8,128)S(1)}, s32[]{:T(128)}, s32[]{:T(128)}, s32[]{:T(128)}, /*index=5*/s32[]{:T(128)}) while((s32[]{:T(128)}, f32[16,32]{0,1:T(8,128)S(1)}, s32[]{:T(128)}, s32[]{:T(128)}, s32[]{:T(128)}, /*index=5*/s32[]{:T(128)}) %tuple.340), condition=%wide.region_16.19_spmd.clone, body=%wide.region_15.18_spmd.clone.sunk | while | flops 1108 | bytes 5825 | solution.py:48
  637.1 24.0 %while.142 = (s32[]{:T(128)}, f32[16,32]{0,1:T(8,128)S(1)}, s32[]{:T(128)}, s32[]{:T(128)}, s32[]{:T(128)}, /*index=5*/s32[]{:T(128)}) while((s32[]{:T(128)}, f32[16,32]{0,1:T(8,128)S(1)}, s32[]{:T(128)}, s32[]{:T(128)}, s32[]{:T(128)}, /*index=5*/s32[]{:T(128)}) %tuple.343), condition=%wide.region_18.21_spmd.clone, body=%wide.region_17.20_spmd.clone.sunk | while | flops 1108 | bytes 5825 | solution.py:48
  661.7 24.0 %while.143 = (s32[]{:T(128)}, f32[16,32]{0,1:T(8,128)S(1)}, s32[]{:T(128)}, s32[]{:T(128)}, s32[]{:T(128)}, /*index=5*/s32[]{:T(128)}) while((s32[]{:T(128)}, f32[16,32]{0,1:T(8,128)S(1)}, s32[]{:T(128)}, s32[]{:T(128)}, s32[]{:T(128)}, /*index=5*/s32[]{:T(128)}) %tuple.346), condition=%wide.region_20.23_spmd.clone, body=%wide.region_19.22_spmd.clone.sunk | while | flops 1108 | bytes 5825 | solution.py:48
  687.2 6.9 convolution_bitcast_fusion
  694.1 5.0 collective-permute-start
  700.3 1.3 collective-permute-start.1
  702.0 5.9 collective-permute-done.1
  707.9 2.8 collective-permute-start.2
  711.2 5.0 collective-permute-done.2
  716.8 1.0 fusion.137
  718.2 136.5 %all-reduce.11.cloned.1.call-done = f32[128,128]{1,0:T(8,128)} async-done(((f32[128,128]{1,0:T(8,128)}), f32[128,128]{1,0:T(8,128)}) %all-reduce.11.cloned.1.call-update) | async-done | bytes 65552 | tf_op jit(solution)/shard_map/psum | solution.py:107
  854.7 1.2 fusion.133
  855.9 1.3 fusion.48
  857.2 1.5 convolution_negate_fusion
  858.8 98.6 %all-gather.5.cloned.1.call-done = f32[16384,128]{1,0:T(8,128)} async-done(((f32[512,128]{1,0:T(8,128)}), f32[16384,128]{1,0:T(8,128)}) %all-gather.5.cloned.1.call-update) | async-done | bytes 8388624 | tf_op jit(solution)/shard_map/all_gather | solution.py:110
  957.4 5.0 fusion.49
  962.4 6.7 subtract_subtract_fusion
  (613 shorter events, 199.7 us)
Async XLA Ops:
  7.2 1.0 copy-start
  7.2 145.8 %all-reduce.5.cloned.1.call-start = ((), (), s32[]{:S(2)}) async-start(), calls=%async_computation | async-start | bytes 131072 | tf_op jit(solution)/shard_map/psum | solution.py:86
  9.4 309.4 %all-reduce.7.cloned.1.call-start = ((), (), s32[]{:S(2)}) async-start(), calls=%async_computation.1 | async-start | bytes 131072 | tf_op jit(solution)/shard_map/psum | solution.py:89
  167.8 689.5 %copy-start.4 = (f32[128,128]{1,0:T(8,128)}, f32[128,128]{1,0:T(8,128)S(1)}, u32[]{:S(2)}) copy-start(f32[128,128]{1,0:T(8,128)S(1)} %get-tuple-element.926) | copy-start | bytes 196612
  179.1 305.8 %all-reduce.9.cloned.1.call-start = ((), (), s32[]{:S(2)}) async-start(), calls=%async_computation.3 | async-start | bytes 131072 | tf_op jit(solution)/shard_map/psum | solution.py:11
  345.1 342.0 %all-gather.3.cloned.1.call-start = ((), (), s32[]{:S(2)}) async-start(), calls=%async_computation.2 | async-start | bytes 8650752 | tf_op jit(solution)/shard_map/all_gather | solution.py:98
  345.7 509.0 %all-reduce.11.cloned.1.call-start = ((), (), s32[]{:S(2)}) async-start(), calls=%async_computation.4 | async-start | bytes 131072 | tf_op jit(solution)/shard_map/psum | solution.py:107
  687.1 29.7 %copy-start.2 = (f32[512,128]{0,1:T(8,128)S(1)}, f32[512,128]{0,1:T(8,128)}, u32[]{:S(2)}) copy-start(f32[512,128]{0,1:T(8,128)} %get-tuple-element.927) | copy-start | bytes 786436
  694.1 6.2 collective-permute-start
  700.3 7.6 collective-permute-start.1
  707.9 8.2 collective-permute-start.2
  717.9 239.5 %all-gather.5.cloned.1.call-start = ((), (), s32[]{:S(2)}) async-start(), calls=%async_computation.5 | async-start | bytes 8650752 | tf_op jit(solution)/shard_map/all_gather | solution.py:110
  857.2 105.2 %copy-start.3 = (f32[512,128]{1,0:T(8,128)S(1)}, f32[512,128]{1,0:T(8,128)}, u32[]{:S(2)}) copy-start(f32[512,128]{1,0:T(8,128)} %fusion.48) | copy-start | bytes 786436
  957.4 5.1 copy-start.1
Sparse Core Ops, SparseCore 0:
  12.0 140.8 all-reduce.4
  179.2 139.5 all-reduce.6
  345.3 139.6 all-reduce.8
  487.9 100.0 all-gather.2
  718.0 136.6 all-reduce.10
  857.7 99.5 all-gather.4
